TPU v7x, 32 devices: a whole 2x2x4 slice. The times are simulated.
32 devices in a mesh: groups: 2 (over y), wide: 4 (over x, core), narrow: 4 (over z).
Axes of the slice: x: 2, y: 2, z: 4, core: 2. Of those that a mesh axis runs over, the one named last changes fastest.
Arguments:
- basis: bfloat16 [128, 64, 2, 512], P(('groups', 'wide'), 'narrow'), parts along dimension 0, may hold values from -0.25 to 0.25
- kappa: float32 [128, 64, 2], P(('groups', 'wide'), 'narrow'), parts along dimension 0, may hold values from 0.1 to 1
- velocity: float32 [3, 512], P(None, 'groups'), parts along dimension 1, may hold values from -2 to 2
- coefficients: float32 [512, 512], P('groups'), parts along dimension 0, may hold values from -6 to 6
- propagator: float32 [1024, 512], P('groups'), parts along dimension 0, may hold values from -0.25 to 0.25
Outputs:
- advanced: float32 [512, 512], P(('groups', 'wide', 'narrow')), parts along dimension 0
There are 2 independent parts, one for each index of `groups`. A program takes and returns all parts, laid end to end along the dimension named above; each array names one. Nothing has to cross between parts.
All inputs are finite; a program needn't handle non-finite values.
Results may differ from a plain program's by a relative error of at most 0.0056.
Values may be sent and summed in bfloat16 or wider, within the bound.
No kernel may reach another device: no remote copies, remote signals or barrier semaphores. Data moves between devices by JAX's collectives and lax.ppermute only.
A program may use at most 64 MiB of HBM per device.

v0:
```python
import math

import jax
import jax.numpy as jnp
from jax import lax
from jax.sharding import PartitionSpec as P

ITERS = 2


step_size = 4.0


def padded_2(x, sides, width):
    for axis, dim in sides:
        devices, length = (lax.axis_size(axis), x.shape[dim])
        up = [(i, (i + 1) % devices) for i in range(devices - 1)]
        down = [(j, i) for i, j in up]
        last = lax.slice_in_dim(x, length - width, length, axis=dim)
        first = lax.slice_in_dim(x, 0, width, axis=dim)
        before = lax.ppermute(last, axis, up)
        after = lax.ppermute(first, axis, down)
        x = jnp.concatenate([before, x, after], axis=dim)
    return x


def forcing_of(padded, kappa, velocity):
    center = padded[1:-1, 1:-1, 1:-1].astype(jnp.float32)
    x_next = padded[2:, 1:-1, 1:-1].astype(jnp.float32)
    x_prev = padded[:-2, 1:-1, 1:-1].astype(jnp.float32)
    y_next = padded[1:-1, 2:, 1:-1].astype(jnp.float32)
    y_prev = padded[1:-1, :-2, 1:-1].astype(jnp.float32)
    z_next = padded[1:-1, 1:-1, 2:].astype(jnp.float32)
    z_prev = padded[1:-1, 1:-1, :-2].astype(jnp.float32)
    spread = x_next + x_prev + y_next + y_prev + z_next + z_prev - 6.0 * center
    carried = velocity[0] * (x_next * x_next - x_prev * x_prev)
    carried = carried + velocity[1] * (y_next * y_next - y_prev * y_prev)
    carried = carried + velocity[2] * (z_next * z_next - z_prev * z_prev)
    result = kappa[..., None] * spread - 0.25 * carried
    return result.astype(jnp.bfloat16)


def advance(state, summed, scale, propagator):
    update = state + step_size * (summed * scale)
    return update + jnp.dot(
        update, propagator.T, precision=lax.Precision.HIGHEST, preferred_element_type=jnp.float32
    )


def body(basis, kappa, velocity, coefficients, propagator):
    size_x, size_y, size_z, modes = basis.shape
    columns = coefficients.shape[0]
    devices = lax.axis_size("wide") * lax.axis_size("narrow")
    owned = columns // devices
    scale = 1.0 / math.sqrt(size_x * size_y * size_z * devices)
    first_row = lax.axis_index(("wide", "narrow")) * owned
    flat_basis = basis.reshape(size_x * size_y * size_z, modes)
    lift_x, lift_y = (size_x, size_y)

    def lift_piece(piece):
        made = lax.dot_general(
            flat_basis, piece, (((1,), (1,)), ((), ())), preferred_element_type=jnp.float32
        )
        return made.astype(jnp.bfloat16)

    state = lax.dynamic_slice_in_dim(coefficients, first_row, owned, 0)
    lifted = lift_piece(coefficients.astype(jnp.bfloat16))
    for step in range(ITERS):
        field = lifted.reshape(lift_x, lift_y, size_z, columns)
        padded = padded_2(field, (("wide", 0), ("narrow", 1)), 1)
        padded = jnp.pad(padded, ((0, 0), (0, 0), (1, 1), (0, 0)))
        forcing = forcing_of(padded, kappa, velocity).reshape(size_x * size_y * size_z, columns)
        partial_rows = lax.psum_scatter(
            lax.dot_general(
                forcing, flat_basis, (((0,), (0,)), ((), ())), preferred_element_type=jnp.float32
            ),
            "wide",
            scatter_dimension=0,
            tiled=True,
        )
        summed = lax.psum_scatter(partial_rows, "narrow", scatter_dimension=0, tiled=True)
        state = advance(state, summed, scale, propagator)
        if step + 1 < ITERS:
            lifted = lift_piece(
                lax.all_gather(state.astype(jnp.bfloat16), ("wide", "narrow"), axis=0, tiled=True)
            )
    return state


def solution(mesh):
    placed = (
        P(("groups", "wide"), "narrow", None, None),
        P(("groups", "wide"), "narrow", None),
        P(None, "groups"),
        P("groups", None),
        P("groups", None),
    )
    return jax.shard_map(
        body,
        mesh=mesh,
        in_specs=placed,
        out_specs=P(("groups", "wide", "narrow"), None),
        check_vma=False,
    )
```

profile of v0, /device:TPU:0, one launch (start us, length us, event | category | flops | bytes accessed | tf_op | source)
XLA Modules:
  0.0 175.8 jit_solution(13818191396235524787)
XLA Ops:
  6.5 1.4 reshape.19
  7.9 0.3 convolution_convert_fusion.1
  8.2 0.0 copy-start.3
  8.3 2.4 %collective-permute-start.1 = (bf16[1,16,2,256]{3,1,2,0:T(8,128)(2,1)S(1)}, bf16[1,16,2,256]{3,1,2,0:T(8,128)(2,1)S(1)}, u32[]{:S(2)}, u32[]{:S(2)}) collective-permute-start(bf16[1,16,2,256]{3,1,2,0:T(8,128)(2,1)S(1)} %copy.41), channel_id=1, source_target_pairs={{0,4},{4,8},{8,12},{1,5},{5,9},{9,13},{2,6},{6,10},{10,14},{3,7},{... | collective-permute-start | bytes 49160 | tf_op jit(solution)/shard_map/ppermute | solution.py:21
  10.7 1.3 collective-permute-start
  12.0 0.1 reshape.20
  12.2 0.0 collective-permute-done.1
  12.2 0.0 copy-start.2
  12.2 0.0 copy-start.4
  12.2 0.1 constant_dynamic-update-slice_fusion.1
  12.3 3.7 %collective-permute-done = bf16[1,16,2,256]{3,1,2,0:T(8,128)(2,1)S(1)} collective-permute-done((bf16[1,16,2,256]{3,1,2,0:T(8,128)(2,1)S(1)}, bf16[1,16,2,256]{3,1,2,0:T(8,128)(2,1)S(1)}, u32[]{:S(2)}, u32[]{:S(2)}) %collective-permute-start) | collective-permute-done | bytes 16416 | tf_op jit(solution)/shard_map/ppermute | solution.py:22
  15.9 0.1 fusion.51
  16.0 1.3 collective-permute-start.2
  17.3 4.5 %collective-permute-start.3 = (bf16[18,1,2,256]{3,1,2,0:T(2,128)(2,1)S(1)}, bf16[18,1,2,256]{3,1,2,0:T(2,128)(2,1)S(1)}, u32[]{:S(2)}, u32[]{:S(2)}) collective-permute-start(bf16[18,1,2,256]{3,1,2,0:T(2,128)(2,1)S(1)} %get-tuple-element.7), channel_id=1, source_target_pairs={{0,1},{1,2},{2,3},{4,5},{5,6},{6,7},{8,9},{9,10},{10,11},{12,13},{... | collective-permute-start | bytes 55304 | tf_op jit(solution)/shard_map/ppermute | solution.py:21
  21.9 1.6 collective-permute-done.3
  23.5 0.3 select_maximum_fusion.2
  23.8 1.9 %convolution_bitcast_fusion.1 = f32[256,512]{1,0:T(8,128)} fusion(bf16[16,16,2,512]{3,2,1,0:T(2,128)(2,1)S(1)} %copy-done.2, bf16[16,16,2,256]{3,1,2,0:T(8,128)(2,1)S(1)} %get-tuple-element.16, bf16[18,18,4,256]{3,1,2,0:T(8,128)(2,1)S(1)} %select_maximum_fusion.2, bf16[18,16,2,256]{3,1,2,0:T(8,128)(2,1)S(1)} %constant_dynamic-update-slice_fusion, ...), kind=kOutput, calls=%fused_computation.4 | convolution fusion | flops 139984896 | bytes 2255872 | tf_op jit(solution)/shard_map/dot_general | solution.py:74
  25.7 0.0 reduce-scatter.5.cloned.1.call-update
  25.7 0.0 reduce-scatter.7.cloned.1.call-start
  25.7 24.7 %reduce-scatter.5.cloned.1.call-done = f32[64,512]{1,0:T(8,128)} async-done(((f32[256,512]{1,0:T(8,128)}), f32[64,512]{1,0:T(8,128)}) %reduce-scatter.5.cloned.1.call-update) | async-done | bytes 131088 | tf_op jit(solution)/shard_map/reduce_scatter | solution.py:73
  50.4 0.0 reduce-scatter.7.cloned.1.call-update
  50.4 0.0 reduce-scatter.9.cloned.1.call-start
  50.5 21.6 %reduce-scatter.7.cloned.1.call-done = f32[16,512]{1,0:T(8,128)} async-done(((f32[64,512]{1,0:T(8,128)}), f32[16,512]{1,0:T(8,128)}) %reduce-scatter.7.cloned.1.call-update) | async-done | bytes 32784 | tf_op jit(solution)/shard_map/reduce_scatter | solution.py:81
  72.1 1.7 fusion.55
  73.9 30.9 %all_gather.3 = bf16[256,512]{1,0:T(8,128)(2,1)S(1)} all-gather(bf16[16,512]{1,0:T(8,128)(2,1)S(1)} %get-tuple-element.20), channel_id=1, replica_groups=mesh['groups'=2,'wide'=4,'narrow'=4] {'wide','narrow'}, dimensions={0}, use_global_device_ids=true | all-gather | bytes 278528 | tf_op jit(solution)/shard_map/all_gather | solution.py:85
  104.7 0.3 fusion.1
  105.1 0.1 fusion.52
  105.2 0.1 copy.50
  105.3 1.3 collective-permute-start.5
  106.6 0.1 copy.46
  106.7 0.1 reshape.21
  106.8 0.1 copy.47
  107.0 1.3 collective-permute-start.4
  108.3 0.0 collective-permute-done.5
  108.3 0.1 constant_dynamic-update-slice_fusion.4
  108.4 3.7 %collective-permute-done.4 = bf16[1,16,2,256]{3,1,2,0:T(8,128)(2,1)S(1)} collective-permute-done((bf16[1,16,2,256]{3,1,2,0:T(8,128)(2,1)S(1)}, bf16[1,16,2,256]{3,1,2,0:T(8,128)(2,1)S(1)}, u32[]{:S(2)}, u32[]{:S(2)}) %collective-permute-start.4) | collective-permute-done | bytes 16416 | tf_op jit(solution)/shard_map/ppermute | solution.py:22
  112.0 0.1 fusion.50
  112.1 1.3 collective-permute-start.6
  113.4 4.5 %collective-permute-start.7 = (bf16[18,1,2,256]{3,1,2,0:T(2,128)(2,1)S(1)}, bf16[18,1,2,256]{3,1,2,0:T(2,128)(2,1)S(1)}, u32[]{:S(2)}, u32[]{:S(2)}) collective-permute-start(bf16[18,1,2,256]{3,1,2,0:T(2,128)(2,1)S(1)} %get-tuple-element.5), channel_id=1, source_target_pairs={{0,1},{1,2},{2,3},{4,5},{5,6},{6,7},{8,9},{9,10},{10,11},{12,13},{... | collective-permute-start | bytes 55304 | tf_op jit(solution)/shard_map/ppermute | solution.py:21
  118.0 1.6 collective-permute-done.7
  119.6 0.3 select_maximum_fusion
  119.9 1.9 %convolution_bitcast_fusion = f32[256,512]{1,0:T(8,128)} fusion(bf16[16,16,2,512]{3,2,1,0:T(2,128)(2,1)S(1)} %copy-done.2, bf16[16,16,2,256]{3,1,2,0:T(8,128)(2,1)S(1)} %get-tuple-element.12, bf16[18,18,4,256]{3,1,2,0:T(8,128)(2,1)S(1)} %select_maximum_fusion, bf16[18,16,2,256]{3,1,2,0:T(8,128)(2,1)S(1)} %constant_dynamic-update-slice_fusion.3, ...), kind=kOutput, calls=%fused_computation.3 | convolution fusion | flops 139984896 | bytes 2255872 | tf_op jit(solution)/shard_map/dot_general | solution.py:74
  121.8 0.0 reduce-scatter.9.cloned.1.call-update
  121.8 0.0 reduce-scatter.11.cloned.1.call-start
  121.8 23.6 %reduce-scatter.9.cloned.1.call-done = f32[64,512]{1,0:T(8,128)} async-done(((f32[256,512]{1,0:T(8,128)}), f32[64,512]{1,0:T(8,128)}) %reduce-scatter.9.cloned.1.call-update) | async-done | bytes 131088 | tf_op jit(solution)/shard_map/reduce_scatter | solution.py:73
  145.4 0.0 reduce-scatter.11.cloned.1.call-update
  145.4 21.6 %reduce-scatter.11.cloned.1.call-done = f32[16,512]{1,0:T(8,128)} async-done(((f32[64,512]{1,0:T(8,128)}), f32[16,512]{1,0:T(8,128)}) %reduce-scatter.11.cloned.1.call-update) | async-done | bytes 32784 | tf_op jit(solution)/shard_map/reduce_scatter | solution.py:81
  167.0 2.3 %convolution_add_fusion = f32[16,512]{1,0:T(8,128)} fusion(f32[512,512]{1,0:T(8,128)S(1)} %copy-done, f32[16,512]{1,0:T(8,128)S(1)} %get-tuple-element.21, f32[16,512]{1,0:T(8,128)} %reduce-scatter.11.cloned.1.call-done), kind=kOutput, calls=%fused_computation.8 | convolution fusion | flops 50356224 | bytes 1146880 | tf_op jit(solution)/shard_map/dot_general | solution.py:45
  (24 shorter events, 0.2 us)
Async XLA Ops:
  6.5 65.6 %copy-start = (f32[512,512]{1,0:T(8,128)S(1)}, f32[512,512]{1,0:T(8,128)}, u32[]{:S(2)}) copy-start(f32[512,512]{1,0:T(8,128)} %param.9) | copy-start | bytes 3145732
  6.5 1.4 copy-start.1
  6.5 43.9 %reduce-scatter.5.cloned.1.call-start = ((), (), s32[]{:S(2)}) async-start(), calls=%async_computation.4 | async-start | bytes 655360 | tf_op jit(solution)/shard_map/reduce_scatter | solution.py:73
  8.2 13.6 %copy-start.3 = (f32[3,256]{1,0:T(4,128)S(1)}, f32[3,256]{1,0:T(4,128)}, u32[]{:S(2)}) copy-start(f32[3,256]{1,0:T(4,128)} %param.7) | copy-start | bytes 9220
  8.3 3.9 %collective-permute-start.1 = (bf16[1,16,2,256]{3,1,2,0:T(8,128)(2,1)S(1)}, bf16[1,16,2,256]{3,1,2,0:T(8,128)(2,1)S(1)}, u32[]{:S(2)}, u32[]{:S(2)}) collective-permute-start(bf16[1,16,2,256]{3,1,2,0:T(8,128)(2,1)S(1)} %copy.41), channel_id=1, source_target_pairs={{0,4},{4,8},{8,12},{1,5},{5,9},{9,13},{2,6},{6,10},{10,14},{3,7},{... | collective-permute-start | bytes 49160 | tf_op jit(solution)/shard_map/ppermute | solution.py:21
  10.7 5.2 %collective-permute-start = (bf16[1,16,2,256]{3,1,2,0:T(8,128)(2,1)S(1)}, bf16[1,16,2,256]{3,1,2,0:T(8,128)(2,1)S(1)}, u32[]{:S(2)}, u32[]{:S(2)}) collective-permute-start(bf16[1,16,2,256]{3,1,2,0:T(8,128)(2,1)S(1)} %copy.39), channel_id=1, source_target_pairs={{4,0},{8,4},{12,8},{5,1},{9,5},{13,9},{6,2},{10,6},{14,10},{7,3},{... | collective-permute-start | bytes 49160 | tf_op jit(solution)/shard_map/ppermute | solution.py:22
  12.2 11.6 %copy-start.2 = (bf16[16,16,2,512]{3,2,1,0:T(2,128)(2,1)S(1)}, bf16[16,16,2,512]{3,2,1,0:T(2,128)(2,1)}, u32[]{:S(2)}) copy-start(bf16[16,16,2,512]{3,2,1,0:T(2,128)(2,1)} %param.5) | copy-start | bytes 1572868
  12.2 11.6 %copy-start.4 = (f32[16,16,2]{1,2,0:T(2,128)S(1)}, f32[16,16,2]{1,2,0:T(2,128)}, u32[]{:S(2)}) copy-start(f32[16,16,2]{1,2,0:T(2,128)} %param.6) | copy-start | bytes 6148
  16.0 5.9 %collective-permute-start.2 = (bf16[18,1,2,256]{3,1,2,0:T(2,128)(2,1)S(1)}, bf16[18,1,2,256]{3,1,2,0:T(2,128)(2,1)S(1)}, u32[]{:S(2)}, u32[]{:S(2)}) collective-permute-start(bf16[18,1,2,256]{3,1,2,0:T(2,128)(2,1)S(1)} %get-tuple-element.8), channel_id=1, source_target_pairs={{1,0},{2,1},{3,2},{5,4},{6,5},{7,6},{9,8},{10,9},{11,10},{13,12},{... | collective-permute-start | bytes 55304 | tf_op jit(solution)/shard_map/ppermute | solution.py:22
  17.3 6.2 %collective-permute-start.3 = (bf16[18,1,2,256]{3,1,2,0:T(2,128)(2,1)S(1)}, bf16[18,1,2,256]{3,1,2,0:T(2,128)(2,1)S(1)}, u32[]{:S(2)}, u32[]{:S(2)}) collective-permute-start(bf16[18,1,2,256]{3,1,2,0:T(2,128)(2,1)S(1)} %get-tuple-element.7), channel_id=1, source_target_pairs={{0,1},{1,2},{2,3},{4,5},{5,6},{6,7},{8,9},{9,10},{10,11},{12,13},{... | collective-permute-start | bytes 55304 | tf_op jit(solution)/shard_map/ppermute | solution.py:21
  25.7 46.4 %reduce-scatter.7.cloned.1.call-start = ((), (), s32[]{:S(2)}) async-start(), calls=%async_computation.5 | async-start | bytes 163840 | tf_op jit(solution)/shard_map/reduce_scatter | solution.py:81
  50.4 94.9 %reduce-scatter.9.cloned.1.call-start = ((), (), s32[]{:S(2)}) async-start(), calls=%async_computation.6 | async-start | bytes 655360 | tf_op jit(solution)/shard_map/reduce_scatter | solution.py:73
  105.3 3.0 %collective-permute-start.5 = (bf16[1,16,2,256]{3,1,2,0:T(8,128)(2,1)S(1)}, bf16[1,16,2,256]{3,1,2,0:T(8,128)(2,1)S(1)}, u32[]{:S(2)}, u32[]{:S(2)}) collective-permute-start(bf16[1,16,2,256]{3,1,2,0:T(8,128)(2,1)S(1)} %copy.51), channel_id=1, source_target_pairs={{0,4},{4,8},{8,12},{1,5},{5,9},{9,13},{2,6},{6,10},{10,14},{3,7},{... | collective-permute-start | bytes 49160 | tf_op jit(solution)/shard_map/ppermute | solution.py:21
  107.0 5.1 %collective-permute-start.4 = (bf16[1,16,2,256]{3,1,2,0:T(8,128)(2,1)S(1)}, bf16[1,16,2,256]{3,1,2,0:T(8,128)(2,1)S(1)}, u32[]{:S(2)}, u32[]{:S(2)}) collective-permute-start(bf16[1,16,2,256]{3,1,2,0:T(8,128)(2,1)S(1)} %copy.48), channel_id=1, source_target_pairs={{4,0},{8,4},{12,8},{5,1},{9,5},{13,9},{6,2},{10,6},{14,10},{7,3},{... | collective-permute-start | bytes 49160 | tf_op jit(solution)/shard_map/ppermute | solution.py:22
  112.1 5.9 %collective-permute-start.6 = (bf16[18,1,2,256]{3,1,2,0:T(2,128)(2,1)S(1)}, bf16[18,1,2,256]{3,1,2,0:T(2,128)(2,1)S(1)}, u32[]{:S(2)}, u32[]{:S(2)}) collective-permute-start(bf16[18,1,2,256]{3,1,2,0:T(2,128)(2,1)S(1)} %get-tuple-element.6), channel_id=1, source_target_pairs={{1,0},{2,1},{3,2},{5,4},{6,5},{7,6},{9,8},{10,9},{11,10},{13,12},{... | collective-permute-start | bytes 55304 | tf_op jit(solution)/shard_map/ppermute | solution.py:22
  113.4 6.2 %collective-permute-start.7 = (bf16[18,1,2,256]{3,1,2,0:T(2,128)(2,1)S(1)}, bf16[18,1,2,256]{3,1,2,0:T(2,128)(2,1)S(1)}, u32[]{:S(2)}, u32[]{:S(2)}) collective-permute-start(bf16[18,1,2,256]{3,1,2,0:T(2,128)(2,1)S(1)} %get-tuple-element.5), channel_id=1, source_target_pairs={{0,1},{1,2},{2,3},{4,5},{5,6},{6,7},{8,9},{9,10},{10,11},{12,13},{... | collective-permute-start | bytes 55304 | tf_op jit(solution)/shard_map/ppermute | solution.py:21
  121.8 45.2 %reduce-scatter.11.cloned.1.call-start = ((), (), s32[]{:S(2)}) async-start(), calls=%async_computation.7 | async-start | bytes 163840 | tf_op jit(solution)/shard_map/reduce_scatter | solution.py:81
Sparse Core Ops, SparseCore 0:
  25.8 24.5 reduce-scatter.4
  52.7 19.4 reduce-scatter.6
  121.9 23.4 reduce-scatter.8
  147.5 19.4 reduce-scatter.10
where the time goes:
time: 176 us
  waiting for transfers between devices  102 us (58%)
  blocking collectives  30.9 us (18%)
  starting transfers between devices  18.1 us (10%)
  between operations  13.4 us (8%)
  matrix products  8.48 us (5%)
  local copies, waits for them, and re-layouts  2.33 us (1%)
    reduce_scatter x2, waiting for transfers between devices, body(): lax.psum_scatter(lax.dot_general(forcing, flat_basis, (((0,), (0,)), ((),...  48.2 us
    reduce_scatter x2, waiting for transfers between devices, body(): lax.psum_scatter(partial_rows, 'narrow', scatter_dimension=0, tiled=True)  43.2 us
    all_gather x1, blocking collectives, body(): lax.all_gather(state.astype(jnp.bfloat16), ('wide', 'narrow'), axis=0, ti...  30.9 us
    ppermute x4, starting transfers between devices, padded_2(): before = lax.ppermute(last, axis, up)  12.8 us
    ppermute x4, waiting for transfers between devices, padded_2(): after = lax.ppermute(first, axis, down)  7.34 us
    ppermute x4, starting transfers between devices, padded_2(): after = lax.ppermute(first, axis, down)  5.17 us
    dot_general x2, matrix products, advance(): jnp.dot(update, propagator.T, precision=lax.Precision.HIGHEST, preferred_...  4.07 us
    dot_general x2, matrix products, body(): lax.dot_general(forcing, flat_basis, (((0,), (0,)), ((), ())), preferred_...  3.75 us
  transfers between devices with their start and end apart: 12, of which 8 were waited for; matrix products, arithmetic and copies ran while one was open for 0% of the time, Pallas kernels for 0%

commit v1 on v0

v1 whole, which is shorter than its diff:
```python
import functools
import math

import jax
import jax.numpy as jnp
from jax import lax
from jax.experimental import pallas as pl
from jax.experimental.pallas import tpu as pltpu
from jax.sharding import PartitionSpec as P

ITERS = 2
STEP_SIZE = 4.0
F32 = jnp.float32
BF16 = jnp.bfloat16
NT = (((1,), (1,)), ((), ()))
TN = (((0,), (0,)), ((), ()))


def swap(x, axis, distance):
    devices = lax.axis_size(axis)
    return lax.ppermute(x, axis, [(i, i ^ distance) for i in range(devices)])


def gather(x, axis):
    blocks = {0: x}
    distance = lax.axis_size(axis) // 2
    while distance:
        blocks.update({r | distance: swap(block, axis, distance) for r, block in list(blocks.items())})
        distance //= 2
    return [blocks[r] for r in range(len(blocks))]


def split(x):
    high = x.astype(BF16)
    return high, (x - high.astype(F32)).astype(BF16)


def apply_propagator(update, high_ref, low_ref):
    high, low = split(update)
    made = lax.dot_general(high, high_ref[...], NT, preferred_element_type=F32)
    made += lax.dot_general(high, low_ref[...], NT, preferred_element_type=F32)
    made += lax.dot_general(low, high_ref[...], NT, preferred_element_type=F32)
    return update + made


def project(state, place_ref, mains, halos, kappas, velocity_ref, dims, pair_ref, lifted_ref, kappa_ref, forcing_ref):
    size_y, size_x, samples, modes = dims
    wide = len(mains)
    span = wide * size_x
    lanes = 2 * samples
    rounded = state.astype(BF16)
    nothing = jnp.zeros((samples, modes), BF16)
    pair_ref[pl.ds(0, samples), pl.ds(0, modes)] = rounded
    pair_ref[pl.ds(0, samples), pl.ds(modes, modes)] = nothing
    pair_ref[pl.ds(samples, samples), pl.ds(0, modes)] = nothing
    pair_ref[pl.ds(samples, samples), pl.ds(modes, modes)] = rounded
    pair = pair_ref[...]
    lower = lax.broadcasted_iota(jnp.int32, (size_y * size_x, lanes), 1) < samples
    starts = []
    for r in range(wide):
        start = pl.multiple_of((place_ref[0] ^ r) * size_x, size_x)
        starts.append(start)
        rows = pl.ds(start, size_x)
        made = lax.dot_general(mains[r][...], pair, NT, preferred_element_type=F32).astype(BF16).astype(F32)
        lifted_ref[pl.ds(1, size_y), rows, :] = made.reshape(size_y, size_x, lanes)
        made = lax.dot_general(halos[r][...], pair, NT, preferred_element_type=F32).astype(BF16).astype(F32)
        lifted_ref[0, rows, :] = made[:size_x]
        lifted_ref[size_y + 1, rows, :] = made[size_x:]
        cells = jnp.where(lower, kappas[r][:, 0:1], kappas[r][:, 1:2])
        kappa_ref[:, rows, :] = cells.reshape(size_y, size_x, lanes)
    place = lax.broadcasted_iota(jnp.int32, (span, lanes), 0)
    first, last = place == 0, place == span - 1
    speed_x, speed_y, speed_z = (velocity_ref[pl.ds(d, 1), :] for d in range(3))
    for y in range(size_y):
        center = lifted_ref[y + 1]
        y_prev, y_next = lifted_ref[y], lifted_ref[y + 2]
        x_prev = jnp.where(first, 0.0, pltpu.roll(center, 1, 0))
        x_next = jnp.where(last, 0.0, pltpu.roll(center, span - 1, 0))
        other = pltpu.roll(center, samples, 1)
        spread = x_next + x_prev + y_next + y_prev + other - 6.0 * center
        carried = speed_x * (x_next * x_next - x_prev * x_prev)
        carried = carried + speed_y * (y_next * y_next - y_prev * y_prev)
        carried = carried + speed_z * (other * other)
        forcing_ref[y] = (kappa_ref[y] * spread - carried).astype(BF16)
    total = None
    for r in range(wide):
        forcing = forcing_ref[:, pl.ds(starts[r], size_x), :].reshape(size_y * size_x, lanes)
        turned = forcing.T
        for z in range(2):
            made = jnp.dot(
                turned[z * samples : (z + 1) * samples],
                mains[r][:, pl.ds(z * modes, modes)],
                preferred_element_type=F32,
            )
            total = made if total is None else total + made
    return total


def first_kernel(dims, wide, place_ref, *refs):
    mains, halos, kappas = (refs[i * wide : (i + 1) * wide] for i in range(3))
    velocity_ref, state_ref, total_ref, sent_ref = refs[3 * wide : 3 * wide + 4]
    total = project(state_ref[...], place_ref, mains, halos, kappas, velocity_ref, dims, *refs[3 * wide + 4 :])
    total_ref[...] = total
    sent_ref[...] = total.astype(BF16)


def next_kernel(dims, wide, factor, half, place_ref, *refs):
    mains, halos, kappas = (refs[i * wide : (i + 1) * wide] for i in range(3))
    velocity_ref, state_ref, high_ref, low_ref, mine_ref, other_ref, new_ref, kept_ref, sent_ref = refs[3 * wide : 3 * wide + 9]
    update = state_ref[...] + factor * (mine_ref[...] + other_ref[...].astype(F32))
    state = apply_propagator(update, high_ref, low_ref)
    new_ref[...] = state
    total_ref = refs[-1]
    total_ref[...] = project(state, place_ref, mains, halos, kappas, velocity_ref, dims, *refs[3 * wide + 9 : -1])
    kept_ref[...] = total_ref[pl.ds(pl.multiple_of(place_ref[1] * half, half), half), :]
    sent_ref[...] = total_ref[pl.ds(pl.multiple_of((1 - place_ref[1]) * half, half), half), :].astype(BF16)


def last_kernel(factor, state_ref, high_ref, low_ref, mine_ref, other_ref, out_ref):
    update = state_ref[...] + factor * (mine_ref[...] + other_ref[...].astype(F32))
    out_ref[...] = apply_propagator(update, high_ref, low_ref)


def body(basis, kappa, velocity, coefficients, propagator):
    size_x, size_y, size_z, modes = basis.shape
    columns = coefficients.shape[0]
    wide, narrow = lax.axis_size("wide"), lax.axis_size("narrow")
    owned = columns // (wide * narrow)
    real = owned * narrow
    samples = -(-real // 64) * 64
    factor = STEP_SIZE / math.sqrt(size_x * size_y * size_z * wide * narrow)
    w, n = lax.axis_index("wide"), lax.axis_index("narrow")

    cells = basis.transpose(1, 0, 2, 3).reshape(size_y, size_x, size_z * modes)
    up = [(i, i + 1) for i in range(narrow - 1)]
    down = [(j, i) for i, j in up]
    mains = gather(cells.reshape(size_y * size_x, size_z * modes), "wide")
    halo = jnp.concatenate(
        [lax.ppermute(cells[size_y - 1], "narrow", up), lax.ppermute(cells[0], "narrow", down)], axis=0
    )
    halos = gather(halo, "wide")
    kappas = gather(kappa.transpose(1, 0, 2).reshape(size_y * size_x, size_z), "wide")

    def padded(x):
        return x if real == samples else jnp.pad(x, ((0, samples - real), (0, 0)))

    state = padded(lax.dynamic_slice_in_dim(coefficients, w * real, real, 0))
    speed = 0.25 * lax.dynamic_slice_in_dim(velocity, w * real, real, 1)
    if real != samples:
        speed = jnp.pad(speed, ((0, 0), (0, samples - real)))
    speed = jnp.concatenate([speed, speed * jnp.array([[1.0], [1.0], [-1.0]], F32)], axis=1)
    high = lax.reduce_precision(propagator, 8, 7)
    low = (propagator - high).astype(BF16)
    high = high.astype(BF16)

    dims = (size_y, size_x, samples, modes)
    span = wide * size_x
    scratch = [
        pltpu.VMEM((2 * samples, size_z * modes), BF16),
        pltpu.VMEM((size_y + 2, span, 2 * samples), F32),
        pltpu.VMEM((size_y, span, 2 * samples), F32),
        pltpu.VMEM((size_y, span, 2 * samples), BF16),
    ]
    smem = pl.BlockSpec(memory_space=pltpu.SMEM)
    vmem = pl.BlockSpec(memory_space=pltpu.VMEM)
    half = real // 2
    top = narrow // 2
    place = jnp.stack([w, n // top]).astype(jnp.int32)
    fixed = (*mains, *halos, *kappas, speed)

    total, sent = pl.pallas_call(
        functools.partial(first_kernel, dims, wide),
        out_shape=(jax.ShapeDtypeStruct((samples, modes), F32), jax.ShapeDtypeStruct((samples, modes), BF16)),
        in_specs=[smem] + [vmem] * (len(fixed) + 1),
        out_specs=(vmem, vmem),
        scratch_shapes=scratch,
    )(place, *fixed, state)
    distance = 1
    while distance < top:
        total = total + swap(sent, "narrow", distance).astype(F32)
        sent = total.astype(BF16)
        distance *= 2
    got = swap(sent, "narrow", top)
    state, total, sent = pl.pallas_call(
        functools.partial(next_kernel, dims, wide, factor, half),
        out_shape=(
            jax.ShapeDtypeStruct((samples, modes), F32),
            jax.ShapeDtypeStruct((half, modes), F32),
            jax.ShapeDtypeStruct((half, modes), BF16),
        ),
        in_specs=[smem] + [vmem] * (len(fixed) + 5),
        out_specs=(vmem, vmem, vmem),
        scratch_shapes=scratch + [pltpu.VMEM((samples, modes), F32)],
    )(place, *fixed, state, high, low, total, got)
    distance = top
    while distance > 1:
        total = total + swap(sent, "narrow", distance).astype(F32)
        distance //= 2
        rows = total.shape[0] // 2
        bit = (n // distance) % 2
        sent = lax.dynamic_slice_in_dim(total, (1 - bit) * rows, rows, 0).astype(BF16)
        total = lax.dynamic_slice_in_dim(total, bit * rows, rows, 0)
    got = swap(sent, "narrow", 1)
    state = lax.dynamic_slice_in_dim(state, n * owned, owned, 0)
    room = max(owned, 16)
    state, total, got = (
        x if room == owned else jnp.pad(x, ((0, room - owned), (0, 0))) for x in (state, total, got)
    )
    out = pl.pallas_call(
        functools.partial(last_kernel, factor),
        out_shape=jax.ShapeDtypeStruct((room, modes), F32),
        in_specs=[vmem] * 5,
        out_specs=vmem,
    )(state, high, low, total, got)
    return out[:owned]


def solution(mesh):
    placed = (
        P(("groups", "wide"), "narrow", None, None),
        P(("groups", "wide"), "narrow", None),
        P(None, "groups"),
        P("groups", None),
        P("groups", None),
    )
    return jax.shard_map(
        body,
        mesh=mesh,
        in_specs=placed,
        out_specs=P(("groups", "wide", "narrow"), None),
        check_vma=False,
    )
```

time: 176 us -> 65.5 us (0.37)
  waiting for transfers between devices: 102 us -> 17.8 us
  blocking collectives: 30.9 us -> 0 us
  between operations: 13.4 us -> 0.25 us
  Pallas kernels: 0 us -> 12.1 us
  matrix products: 8.48 us -> 0 us
  local copies, waits for them, and re-layouts: 2.33 us -> 8.8 us
  other arithmetic: 0.61 us -> 5.35 us
  starting transfers between devices: 18.1 us -> 20.7 us
    reduce_scatter x4 -> x0, waiting for transfers between devices: 91.4 us -> none  [the longest x2 48.2 us: body(): lax.psum_scatter(lax.dot_general(forcing, flat_basis, (((0,), (0,)), ((),...]
    all_gather x1 -> x0, blocking collectives: 30.9 us -> none  [body(): lax.all_gather(state.astype(jnp.bfloat16), ('wide', 'narrow'), axis=0, ti...]
    pallas_call x0 -> x3, Pallas kernels: none -> 12.1 us  [the longest x1 5.35 us: body(): pl.pallas_call(functools.partial(next_kernel, dims, wide, factor, half),...]
    dot_general x6 -> x0, matrix products: 8.48 us -> none  [the longest x2 4.07 us: advance(): jnp.dot(update, propagator.T, precision=lax.Precision.HIGHEST, preferred_...]
    ppermute x8 -> x15, waiting for transfers between devices: 10.5 us -> 17.8 us  [the longest x13 13.1 us: swap(): return lax.ppermute(x, axis, [(i, i ^ distance) for i in range(devices)])]
    convert_element_type x0 -> x2, other arithmetic: none -> 3.97 us  [the longest x1 2.4 us: body(): low = (propagator - high).astype(BF16)]
    unnamed x14 -> x42, local copies, waits for them, and re-layouts: 0.15 us -> 3.53 us
    ppermute x8 -> x15, starting transfers between devices: 18 us -> 20.7 us  [the longest x13 15.9 us: swap(): return lax.ppermute(x, axis, [(i, i ^ distance) for i in range(devices)])]
  transfers between devices with their start and end apart: 12 -> 15, of which waited for: 8 -> 7; matrix products, arithmetic and copies ran while one was open for 0% -> 11% of each run, Pallas kernels for 0% -> 0%
where the time goes in v1:
time: 65.5 us; the launch traced here: 65 us
  starting transfers between devices  20.7 us (32%)
  waiting for transfers between devices  17.8 us (27%)
  Pallas kernels  12.1 us (18%)
  local copies, waits for them, and re-layouts  8.8 us (13%)
  other arithmetic  5.35 us (8%)
    ppermute x13, starting transfers between devices, swap(): return lax.ppermute(x, axis, [(i, i ^ distance) for i in range(devices)])  15.9 us
    ppermute x13, waiting for transfers between devices, swap(): return lax.ppermute(x, axis, [(i, i ^ distance) for i in range(devices)])  13.1 us
    pallas_call x1, Pallas kernels, body(): pl.pallas_call(functools.partial(next_kernel, dims, wide, factor, half),...  5.35 us
    ppermute x1, waiting for transfers between devices, body(): lax.ppermute(cells[0], 'narrow', down)  4.69 us
    pallas_call x1, Pallas kernels, body(): pl.pallas_call(functools.partial(first_kernel, dims, wide), out_shape=(ja...  4.42 us
    unnamed x42, local copies, waits for them, and re-layouts  3.53 us
    ppermute x1, starting transfers between devices, body(): lax.ppermute(cells[size_y - 1], 'narrow', up)  3.48 us
    convert_element_type x1, other arithmetic, body(): low = (propagator - high).astype(BF16)  2.4 us
  transfers between devices with their start and end apart: 15, of which 7 were waited for; matrix products, arithmetic and copies ran while one was open for 11% of the time, Pallas kernels for 0%

profile of v1, /device:TPU:0, one launch (start us, length us, event | category | flops | bytes accessed | tf_op | source)
XLA Modules:
  0.0 65.0 jit_solution(10911695661214982768)
XLA Ops:
  0.0 1.6 %copy.7 = bf16[16,16,2,512]{3,2,1,0:T(2,128)(2,1)S(1)} copy(bf16[16,16,2,512]{3,2,0,1:T(2,128)(2,1)} %bitcast.25) | data formatting | bytes 1048576 | tf_op jit(solution)/shard_map/transpose | solution.py:134
  1.6 0.0 copy-start.16
  1.6 0.1 copy.9
  1.7 3.0 %collective-permute-start.1 = (bf16[256,1024]{1,0:T(8,128)(2,1)S(1)}, bf16[256,1024]{1,0:T(8,128)(2,1)S(1)}, u32[]{:S(2)}, u32[]{:S(2)}) collective-permute-start(bf16[256,1024]{1,0:T(8,128)(2,1)S(1)} %bitcast.16), channel_id=1, source_target_pairs={{0,8},{4,12},{8,0},{12,4},{1,9},{5,13},{9,1},{13,5},{2,10},{6,14},... | collective-permute-start | bytes 1572872 | tf_op jit(solution)/shard_map/ppermute | solution.py:21
  4.7 0.2 copy.8
  4.9 0.6 collective-permute-start.9
  5.5 0.0 collective-permute-start.8
  5.5 0.5 collective-permute-start
  6.0 0.8 %fusion.2 = (bf16[1,16,2,512]{3,2,0,1:T(2,128)(2,1)S(1)}, bf16[1,16,2,512]{3,2,0,1:T(2,128)(2,1)S(1)}) fusion(bf16[16,16,2,512]{3,2,0,1:T(2,128)(2,1)} %bitcast.26), kind=kLoop, calls=%fused_computation.16 | loop fusion | bytes 131072 | tf_op jit(solution)/shard_map/slice | solution.py:139
  6.9 3.5 %collective-permute-start.3 = (bf16[16,1024]{1,0:T(8,128)(2,1)S(1)}, bf16[16,1024]{1,0:T(8,128)(2,1)S(1)}, u32[]{:S(2)}, u32[]{:S(2)}) collective-permute-start(bf16[16,1024]{1,0:T(8,128)(2,1)S(1)} %bitcast.29), channel_id=1, source_target_pairs={{0,1},{1,2},{2,3},{4,5},{5,6},{6,7},{8,9},{9,10},{10,11},{12,13},{... | collective-permute-start | bytes 98312 | tf_op jit(solution)/shard_map/ppermute | solution.py:139
  10.4 0.0 copy-start.17
  10.4 0.0 copy-start.18
  10.4 0.7 %copy-done.17 = f32[3,256]{1,0:T(4,128)S(1)} copy-done((f32[3,256]{1,0:T(4,128)S(1)}, f32[3,256]{1,0:T(4,128)}, u32[]{:S(2)}) %copy-start.17) | copy-done | bytes 3096
  11.1 0.1 dynamic-slice_multiply_fusion.1
  11.1 6.4 %collective-permute-done.1.refs_2_ = bf16[256,1024]{1,0:T(8,128)(2,1)S(1)} collective-permute-done((bf16[256,1024]{1,0:T(8,128)(2,1)S(1)}, bf16[256,1024]{1,0:T(8,128)(2,1)S(1)}, u32[]{:S(2)}, u32[]{:S(2)}) %collective-permute-start.1) | collective-permute-done | bytes 524320 | tf_op jit(solution)/shard_map/ppermute | solution.py:21
  17.5 0.0 collective-permute-start.2
  17.5 0.7 %constant_dynamic-slice_fusion.2.refs_13_ = f32[64,512]{1,0:T(8,128)} fusion(f32[256,512]{1,0:T(8,128)S(1)} %copy-done, s32[]{:T(128)S(6)} %select_n.26), kind=kLoop, calls=%fused_computation.13 | loop fusion | bytes 262148 | tf_op jit(solution)/shard_map/dynamic_slice | solution.py:147
  18.2 1.3 %collective-permute-start.4 = (bf16[16,1024]{1,0:T(8,128)(2,1)S(1)}, bf16[16,1024]{1,0:T(8,128)(2,1)S(1)}, u32[]{:S(2)}, u32[]{:S(2)}) collective-permute-start(bf16[16,1024]{1,0:T(8,128)(2,1)S(1)} %bitcast.30), channel_id=1, source_target_pairs={{1,0},{2,1},{3,2},{5,4},{6,5},{7,6},{9,8},{10,9},{11,10},{13,12},{... | collective-permute-start | bytes 98312 | tf_op jit(solution)/shard_map/ppermute | solution.py:139
  19.5 4.7 %collective-permute-done.4 = bf16[16,1024]{1,0:T(8,128)(2,1)S(1)} collective-permute-done((bf16[16,1024]{1,0:T(8,128)(2,1)S(1)}, bf16[16,1024]{1,0:T(8,128)(2,1)S(1)}, u32[]{:S(2)}, u32[]{:S(2)}) %collective-permute-start.4) | collective-permute-done | bytes 32800 | tf_op jit(solution)/shard_map/ppermute | solution.py:139
  24.2 1.8 %collective-permute-start.6 = (bf16[32,1024]{1,0:T(8,128)(2,1)S(1)}, bf16[32,1024]{1,0:T(8,128)(2,1)S(1)}, u32[]{:S(2)}, u32[]{:S(2)}) collective-permute-start(bf16[32,1024]{1,0:T(8,128)(2,1)S(1)} %constant_dynamic-update-slice_fusion.refs_4_), channel_id=1, source_target_pairs={{0,8},{4,12},{8,0},{12,4},{1,9},{5,13},{9,1},{13,5},{2,10},{6,14},... | collective-permute-start | bytes 196616 | tf_op jit(solution)/shard_map/ppermute | solution.py:21
  26.1 0.6 pad_maximum_fusion.refs_12_
  26.7 0.0 collective-permute-done.8.refs_9_
  26.7 0.5 collective-permute-start.5
  27.2 1.3 %collective-permute-done.6.refs_6_ = bf16[32,1024]{1,0:T(8,128)(2,1)S(1)} collective-permute-done((bf16[32,1024]{1,0:T(8,128)(2,1)S(1)}, bf16[32,1024]{1,0:T(8,128)(2,1)S(1)}, u32[]{:S(2)}, u32[]{:S(2)}) %collective-permute-start.6) | collective-permute-done | bytes 65568 | tf_op jit(solution)/shard_map/ppermute | solution.py:21
  28.5 0.0 collective-permute-start.7
  28.5 0.7 %pad_add_fusion.place_ref = s32[2]{0:T(128)} fusion(s32[1]{0:T(128)} %bitcast.1, s32[1]{0:T(128)} %bitcast), kind=kLoop, calls=%fused_computation.14 | loop fusion | flops 2 | bytes 16 | tf_op jit(solution)/shard_map/stack | solution.py:168
  29.2 0.0 collective-permute-done.10.refs_11_
  29.2 0.0 collective-permute-done.5.refs_5_
  29.2 0.6 collective-permute-done.7.refs_7_
  29.9 0.5 copy-done.12
  30.4 0.2 copy-done.3
  30.6 0.8 %copy-done.4 = bf16[256,1024]{1,0:T(8,128)(2,1)} copy-done((bf16[256,1024]{1,0:T(8,128)(2,1)}, bf16[256,1024]{1,0:T(8,128)(2,1)S(1)}, u32[]{:S(2)}) %copy-start.4) | copy-done | bytes 524312
  31.4 4.4 %shard_map.64 = (f32[64,512]{1,0:T(8,128)}, bf16[64,512]{1,0:T(8,128)(2,1)}) custom-call(s32[2]{0:T(128)} %pad_add_fusion.place_ref, bf16[256,1024]{1,0:T(8,128)(2,1)} %bitcast.18, bf16[256,1024]{1,0:T(8,128)(2,1)} %copy-done.3, bf16[256,1024]{1,0:T(8,128)(2,1)} %copy-done.2, bf16[256,1024]{1,0:T(8,128)(2,1)} %copy-done.4, bf16[32,1024]{1,0:T(8,128)(2,1)} %copy-done.9, ...), custom_call_target="tpu_custom_call" | custom-call | tf_op jit(solution)/shard_map/pallas_call | solution.py:171
  35.8 1.9 %collective-permute-start.11 = (bf16[64,512]{1,0:T(8,128)(2,1)}, bf16[64,512]{1,0:T(8,128)(2,1)S(1)}, u32[]{:S(2)}, u32[]{:S(2)}) collective-permute-start(bf16[64,512]{1,0:T(8,128)(2,1)} %get-tuple-element.11), channel_id=1, source_target_pairs={{0,1},{1,0},{2,3},{3,2},{4,5},{5,4},{6,7},{7,6},{8,9},{9,8},{10,11... | collective-permute-start | bytes 196616 | tf_op jit(solution)/shard_map/ppermute | solution.py:21
  37.7 2.6 %collective-permute-done.11 = bf16[64,512]{1,0:T(8,128)(2,1)S(1)} collective-permute-done((bf16[64,512]{1,0:T(8,128)(2,1)}, bf16[64,512]{1,0:T(8,128)(2,1)S(1)}, u32[]{:S(2)}, u32[]{:S(2)}) %collective-permute-start.11) | collective-permute-done | bytes 65568 | tf_op jit(solution)/shard_map/ppermute | solution.py:21
  40.3 1.6 %fusion.1 = (bf16[64,512]{1,0:T(8,128)(2,1)S(1)}, f32[64,512]{1,0:T(8,128)}) fusion(f32[64,512]{1,0:T(8,128)} %get-tuple-element.10, bf16[64,512]{1,0:T(8,128)(2,1)S(1)} %collective-permute-done.11), kind=kLoop, calls=%fused_computation.15 | loop fusion | flops 98304 | bytes 393216 | tf_op jit(solution)/shard_map/convert_element_type | solution.py:181
  41.9 2.9 %collective-permute-start.12 = (bf16[64,512]{1,0:T(8,128)(2,1)S(1)}, bf16[64,512]{1,0:T(8,128)(2,1)S(1)}, u32[]{:S(2)}, u32[]{:S(2)}) collective-permute-start(bf16[64,512]{1,0:T(8,128)(2,1)S(1)} %get-tuple-element.15), channel_id=1, source_target_pairs={{0,2},{1,3},{2,0},{3,1},{4,6},{5,7},{6,4},{7,5},{8,10},{9,11},{10,... | collective-permute-start | bytes 196616 | tf_op jit(solution)/shard_map/ppermute | solution.py:21
  44.8 2.4 %fusion = (bf16[512,512]{1,0:T(8,128)(2,1)}, bf16[512,512]{1,0:T(8,128)(2,1)}) fusion(f32[512,512]{1,0:T(8,128)} %param.10), kind=kLoop, calls=%fused_computation.2 | loop fusion | flops 1048576 | bytes 2097152 | tf_op jit(solution)/shard_map/convert_element_type | solution.py:153
  47.2 0.6 copy-done.13
  47.8 5.3 %shard_map.65 = (f32[64,512]{1,0:T(8,128)}, f32[32,512]{1,0:T(8,128)}, bf16[32,512]{1,0:T(8,128)(2,1)}) custom-call(s32[2]{0:T(128)} %pad_add_fusion.place_ref, bf16[256,1024]{1,0:T(8,128)(2,1)} %bitcast.19, bf16[256,1024]{1,0:T(8,128)(2,1)} %copy-done.3, bf16[256,1024]{1,0:T(8,128)(2,1)} %copy-done.2, bf16[256,1024]{1,0:T(8,128)(2,1)} %copy-done.4, ...), custom_call_target="tpu_custom_call" | custom-call | tf_op jit(solution)/shard_map/pallas_call | solution.py:184
  53.1 2.8 %collective-permute-start.13 = (bf16[32,512]{1,0:T(8,128)(2,1)}, bf16[32,512]{1,0:T(8,128)(2,1)S(1)}, u32[]{:S(2)}, u32[]{:S(2)}) collective-permute-start(bf16[32,512]{1,0:T(8,128)(2,1)} %get-tuple-element.14), channel_id=1, source_target_pairs={{0,2},{1,3},{2,0},{3,1},{4,6},{5,7},{6,4},{7,5},{8,10},{9,11},{10,... | collective-permute-start | bytes 98312 | tf_op jit(solution)/shard_map/ppermute | solution.py:21
  56.0 1.4 %constant_dynamic-slice_fusion.1.state_ref = f32[16,512]{1,0:T(8,128)} fusion(f32[64,512]{1,0:T(8,128)} %get-tuple-element.12, s32[]{:T(128)S(6)} %select_n.27), kind=kLoop, calls=%fused_computation.12 | loop fusion | bytes 65540 | tf_op jit(solution)/shard_map/dynamic_slice | solution.py:204
  57.3 0.9 %collective-permute-done.13 = bf16[32,512]{1,0:T(8,128)(2,1)S(1)} collective-permute-done((bf16[32,512]{1,0:T(8,128)(2,1)}, bf16[32,512]{1,0:T(8,128)(2,1)S(1)}, u32[]{:S(2)}, u32[]{:S(2)}) %collective-permute-start.13) | collective-permute-done | bytes 32800 | tf_op jit(solution)/shard_map/ppermute | solution.py:21
  58.3 1.8 %collective-permute-start.14 = (bf16[16,512]{1,0:T(8,128)(2,1)S(1)}, bf16[16,512]{1,0:T(8,128)(2,1)S(1)}, u32[]{:S(2)}, u32[]{:S(2)}) collective-permute-start(bf16[16,512]{1,0:T(8,128)(2,1)S(1)} %dynamic-slice_convert_fusion), channel_id=1, source_target_pairs={{0,1},{1,0},{2,3},{3,2},{4,5},{5,4},{6,7},{7,6},{8,9},{9,8},{10,11... | collective-permute-start | bytes 49160 | tf_op jit(solution)/shard_map/ppermute | solution.py:21
  60.1 0.6 constant_dynamic-slice_fusion.mine_ref
  60.7 1.4 %collective-permute-done.14.other_ref = bf16[16,512]{1,0:T(8,128)(2,1)S(1)} collective-permute-done((bf16[16,512]{1,0:T(8,128)(2,1)S(1)}, bf16[16,512]{1,0:T(8,128)(2,1)S(1)}, u32[]{:S(2)}, u32[]{:S(2)}) %collective-permute-start.14) | collective-permute-done | bytes 16416 | tf_op jit(solution)/shard_map/ppermute | solution.py:21
  62.1 0.6 copy-done.15
  62.7 2.4 %shard_map.66 = f32[16,512]{1,0:T(8,128)} custom-call(f32[16,512]{1,0:T(8,128)} %constant_dynamic-slice_fusion.1.state_ref, bf16[512,512]{1,0:T(8,128)(2,1)} %get-tuple-element.18.refs_14_.high_ref, bf16[512,512]{1,0:T(8,128)(2,1)} %get-tuple-element.17.refs_15_.low_ref, f32[16,512]{1,0:T(8,128)} %constant_dynamic-slice_fusion.mine_ref, ...), custom_call_target="tpu_custom_call" | custom-call | tf_op jit(solution)/shard_map/pallas_call | solution.py:209
  (41 shorter events, 0.1 us)
Async XLA Ops:
  0.0 17.5 %copy-start = (f32[256,512]{1,0:T(8,128)S(1)}, f32[256,512]{1,0:T(8,128)}, u32[]{:S(2)}) copy-start(f32[256,512]{1,0:T(8,128)} %param.9) | copy-start | bytes 1572868
  1.6 3.1 %copy-start.16 = (f32[16,16,2]{1,2,0:T(2,128)S(1)}, f32[16,16,2]{1,2,0:T(2,128)}, u32[]{:S(2)}) copy-start(f32[16,16,2]{1,2,0:T(2,128)} %param.7) | copy-start | bytes 6148
  1.7 28.1 %copy-start.1 = (bf16[32,8,2,512]{3,1,2,0:T(8,128)(2,1)}, bf16[32,8,2,512]{3,1,2,0:T(8,128)(2,1)S(1)}, u32[]{:S(2)}) copy-start(bf16[32,8,2,512]{3,1,2,0:T(8,128)(2,1)S(1)} %copy.9) | copy-start | bytes 1572868
  1.7 15.8 %collective-permute-start.1 = (bf16[256,1024]{1,0:T(8,128)(2,1)S(1)}, bf16[256,1024]{1,0:T(8,128)(2,1)S(1)}, u32[]{:S(2)}, u32[]{:S(2)}) collective-permute-start(bf16[256,1024]{1,0:T(8,128)(2,1)S(1)} %bitcast.16), channel_id=1, source_target_pairs={{0,8},{4,12},{8,0},{12,4},{1,9},{5,13},{9,1},{13,5},{2,10},{6,14},... | collective-permute-start | bytes 1572872 | tf_op jit(solution)/shard_map/ppermute | solution.py:21
  4.9 24.9 %copy-start.5 = (f32[16,16,2]{2,1,0:T(8,128)}, f32[16,16,2]{2,1,0:T(8,128)S(1)}, u32[]{:S(2)}) copy-start(f32[16,16,2]{2,1,0:T(8,128)S(1)} %copy.8) | copy-start | bytes 6148
  4.9 21.8 %collective-permute-start.9 = (f32[256,2]{1,0:T(8,128)S(1)}, f32[256,2]{1,0:T(8,128)S(1)}, u32[]{:S(2)}, u32[]{:S(2)}) collective-permute-start(f32[256,2]{1,0:T(8,128)S(1)} %bitcast.21), channel_id=1, source_target_pairs={{0,8},{4,12},{8,0},{12,4},{1,9},{5,13},{9,1},{13,5},{2,10},{6,14},... | collective-permute-start | bytes 6152 | tf_op jit(solution)/shard_map/ppermute | solution.py:21
  5.5 21.2 %collective-permute-start.8 = (f32[256,2]{1,0:T(8,128)S(1)}, f32[256,2]{1,0:T(8,128)S(1)}, u32[]{:S(2)}, u32[]{:S(2)}) collective-permute-start(f32[256,2]{1,0:T(8,128)S(1)} %bitcast.22), channel_id=1, source_target_pairs={{0,4},{4,0},{8,12},{12,8},{1,5},{5,1},{9,13},{13,9},{2,6},{6,2},{1... | collective-permute-start | bytes 6152 | tf_op jit(solution)/shard_map/ppermute | solution.py:21
  5.5 24.2 %collective-permute-start = (bf16[256,1024]{1,0:T(8,128)(2,1)S(1)}, bf16[256,1024]{1,0:T(8,128)(2,1)S(1)}, u32[]{:S(2)}, u32[]{:S(2)}) collective-permute-start(bf16[256,1024]{1,0:T(8,128)(2,1)S(1)} %bitcast.17), channel_id=1, source_target_pairs={{0,4},{4,0},{8,12},{12,8},{1,5},{5,1},{9,13},{13,9},{2,6},{6,2},{1... | collective-permute-start | bytes 1572872 | tf_op jit(solution)/shard_map/ppermute | solution.py:21
  6.9 11.4 %collective-permute-start.3 = (bf16[16,1024]{1,0:T(8,128)(2,1)S(1)}, bf16[16,1024]{1,0:T(8,128)(2,1)S(1)}, u32[]{:S(2)}, u32[]{:S(2)}) collective-permute-start(bf16[16,1024]{1,0:T(8,128)(2,1)S(1)} %bitcast.29), channel_id=1, source_target_pairs={{0,1},{1,2},{2,3},{4,5},{5,6},{6,7},{8,9},{9,10},{10,11},{12,13},{... | collective-permute-start | bytes 98312 | tf_op jit(solution)/shard_map/ppermute | solution.py:139
  10.4 0.7 %copy-start.17 = (f32[3,256]{1,0:T(4,128)S(1)}, f32[3,256]{1,0:T(4,128)}, u32[]{:S(2)}) copy-start(f32[3,256]{1,0:T(4,128)} %param.8) | copy-start | bytes 9220
  10.4 0.7 %copy-start.18 = (f32[3]{0:T(128)S(1)}, f32[3]{0:T(128)}, u32[]{:S(2)}) copy-start(f32[3]{0:T(128)} %constant.55) | copy-start | bytes 40
  17.5 12.3 %copy-start.2 = (bf16[256,1024]{1,0:T(8,128)(2,1)}, bf16[256,1024]{1,0:T(8,128)(2,1)S(1)}, u32[]{:S(2)}) copy-start(bf16[256,1024]{1,0:T(8,128)(2,1)S(1)} %collective-permute-done.1.refs_2_) | copy-start | bytes 1572868
  17.5 12.3 %collective-permute-start.2 = (bf16[256,1024]{1,0:T(8,128)(2,1)S(1)}, bf16[256,1024]{1,0:T(8,128)(2,1)S(1)}, u32[]{:S(2)}, u32[]{:S(2)}) collective-permute-start(bf16[256,1024]{1,0:T(8,128)(2,1)S(1)} %collective-permute-done.1.refs_2_), channel_id=1, source_target_pairs={{0,4},{4,0},{8,12},{12,8},{1,5},{5,1},{9,13},{13,9},{2,6},{6,2},{1... | collective-permute-start | bytes 1572872 | tf_op jit(solution)/shard_map/ppermute | solution.py:21
  18.2 6.0 %collective-permute-start.4 = (bf16[16,1024]{1,0:T(8,128)(2,1)S(1)}, bf16[16,1024]{1,0:T(8,128)(2,1)S(1)}, u32[]{:S(2)}, u32[]{:S(2)}) collective-permute-start(bf16[16,1024]{1,0:T(8,128)(2,1)S(1)} %bitcast.30), channel_id=1, source_target_pairs={{1,0},{2,1},{3,2},{5,4},{6,5},{7,6},{9,8},{10,9},{11,10},{13,12},{... | collective-permute-start | bytes 98312 | tf_op jit(solution)/shard_map/ppermute | solution.py:139
  24.2 5.6 %copy-start.9 = (bf16[32,1024]{1,0:T(8,128)(2,1)}, bf16[32,1024]{1,0:T(8,128)(2,1)S(1)}, u32[]{:S(2)}) copy-start(bf16[32,1024]{1,0:T(8,128)(2,1)S(1)} %constant_dynamic-update-slice_fusion.refs_4_) | copy-start | bytes 196612
  24.2 4.3 %collective-permute-start.6 = (bf16[32,1024]{1,0:T(8,128)(2,1)S(1)}, bf16[32,1024]{1,0:T(8,128)(2,1)S(1)}, u32[]{:S(2)}, u32[]{:S(2)}) collective-permute-start(bf16[32,1024]{1,0:T(8,128)(2,1)S(1)} %constant_dynamic-update-slice_fusion.refs_4_), channel_id=1, source_target_pairs={{0,8},{4,12},{8,0},{12,4},{1,9},{5,13},{9,1},{13,5},{2,10},{6,14},... | collective-permute-start | bytes 196616 | tf_op jit(solution)/shard_map/ppermute | solution.py:21
  26.7 3.1 %copy-start.6 = (f32[256,2]{1,0:T(8,128)}, f32[256,2]{1,0:T(8,128)S(1)}, u32[]{:S(2)}) copy-start(f32[256,2]{1,0:T(8,128)S(1)} %collective-permute-done.9.refs_10_) | copy-start | bytes 6148
  26.7 2.4 %collective-permute-start.10 = (f32[256,2]{1,0:T(8,128)S(1)}, f32[256,2]{1,0:T(8,128)S(1)}, u32[]{:S(2)}, u32[]{:S(2)}) collective-permute-start(f32[256,2]{1,0:T(8,128)S(1)} %collective-permute-done.9.refs_10_), channel_id=1, source_target_pairs={{0,4},{4,0},{8,12},{12,8},{1,5},{5,1},{9,13},{13,9},{2,6},{6,2},{1... | collective-permute-start | bytes 6152 | tf_op jit(solution)/shard_map/ppermute | solution.py:21
  26.7 3.1 %copy-start.7 = (f32[256,2]{1,0:T(8,128)}, f32[256,2]{1,0:T(8,128)S(1)}, u32[]{:S(2)}) copy-start(f32[256,2]{1,0:T(8,128)S(1)} %collective-permute-done.8.refs_9_) | copy-start | bytes 6148
  26.7 2.4 %collective-permute-start.5 = (bf16[32,1024]{1,0:T(8,128)(2,1)S(1)}, bf16[32,1024]{1,0:T(8,128)(2,1)S(1)}, u32[]{:S(2)}, u32[]{:S(2)}) collective-permute-start(bf16[32,1024]{1,0:T(8,128)(2,1)S(1)} %constant_dynamic-update-slice_fusion.refs_4_), channel_id=1, source_target_pairs={{0,4},{4,0},{8,12},{12,8},{1,5},{5,1},{9,13},{13,9},{2,6},{6,2},{1... | collective-permute-start | bytes 196616 | tf_op jit(solution)/shard_map/ppermute | solution.py:21
  28.5 1.3 %copy-start.10 = (bf16[32,1024]{1,0:T(8,128)(2,1)}, bf16[32,1024]{1,0:T(8,128)(2,1)S(1)}, u32[]{:S(2)}) copy-start(bf16[32,1024]{1,0:T(8,128)(2,1)S(1)} %collective-permute-done.6.refs_6_) | copy-start | bytes 196612
  28.5 1.3 %collective-permute-start.7 = (bf16[32,1024]{1,0:T(8,128)(2,1)S(1)}, bf16[32,1024]{1,0:T(8,128)(2,1)S(1)}, u32[]{:S(2)}, u32[]{:S(2)}) collective-permute-start(bf16[32,1024]{1,0:T(8,128)(2,1)S(1)} %collective-permute-done.6.refs_6_), channel_id=1, source_target_pairs={{0,4},{4,0},{8,12},{12,8},{1,5},{5,1},{9,13},{13,9},{2,6},{6,2},{1... | collective-permute-start | bytes 196616 | tf_op jit(solution)/shard_map/ppermute | solution.py:21
  29.2 0.7 %copy-start.8 = (f32[256,2]{1,0:T(8,128)}, f32[256,2]{1,0:T(8,128)S(1)}, u32[]{:S(2)}) copy-start(f32[256,2]{1,0:T(8,128)S(1)} %collective-permute-done.10.refs_11_) | copy-start | bytes 6148
  29.2 0.7 %copy-start.11 = (bf16[32,1024]{1,0:T(8,128)(2,1)}, bf16[32,1024]{1,0:T(8,128)(2,1)S(1)}, u32[]{:S(2)}) copy-start(bf16[32,1024]{1,0:T(8,128)(2,1)S(1)} %collective-permute-done.5.refs_5_) | copy-start | bytes 196612
  29.8 0.6 copy-start.12
  29.8 0.8 %copy-start.3 = (bf16[256,1024]{1,0:T(8,128)(2,1)}, bf16[256,1024]{1,0:T(8,128)(2,1)S(1)}, u32[]{:S(2)}) copy-start(bf16[256,1024]{1,0:T(8,128)(2,1)S(1)} %collective-permute-done.refs_1_) | copy-start | bytes 1572868
  30.6 0.8 %copy-start.4 = (bf16[256,1024]{1,0:T(8,128)(2,1)}, bf16[256,1024]{1,0:T(8,128)(2,1)S(1)}, u32[]{:S(2)}) copy-start(bf16[256,1024]{1,0:T(8,128)(2,1)S(1)} %collective-permute-done.2.refs_3_) | copy-start | bytes 1572868
  35.8 4.5 %collective-permute-start.11 = (bf16[64,512]{1,0:T(8,128)(2,1)}, bf16[64,512]{1,0:T(8,128)(2,1)S(1)}, u32[]{:S(2)}, u32[]{:S(2)}) collective-permute-start(bf16[64,512]{1,0:T(8,128)(2,1)} %get-tuple-element.11), channel_id=1, source_target_pairs={{0,1},{1,0},{2,3},{3,2},{4,5},{5,4},{6,7},{7,6},{8,9},{9,8},{10,11... | collective-permute-start | bytes 196616 | tf_op jit(solution)/shard_map/ppermute | solution.py:21
  41.9 5.3 %collective-permute-start.12 = (bf16[64,512]{1,0:T(8,128)(2,1)S(1)}, bf16[64,512]{1,0:T(8,128)(2,1)S(1)}, u32[]{:S(2)}, u32[]{:S(2)}) collective-permute-start(bf16[64,512]{1,0:T(8,128)(2,1)S(1)} %get-tuple-element.15), channel_id=1, source_target_pairs={{0,2},{1,3},{2,0},{3,1},{4,6},{5,7},{6,4},{7,5},{8,10},{9,11},{10,... | collective-permute-start | bytes 196616 | tf_op jit(solution)/shard_map/ppermute | solution.py:21
  47.2 0.6 copy-start.13
  53.1 5.1 %copy-start.14 = (f32[32,512]{1,0:T(8,128)S(1)}, f32[32,512]{1,0:T(8,128)}, u32[]{:S(2)}) copy-start(f32[32,512]{1,0:T(8,128)} %get-tuple-element.13) | copy-start | bytes 196612
  53.1 5.1 %collective-permute-start.13 = (bf16[32,512]{1,0:T(8,128)(2,1)}, bf16[32,512]{1,0:T(8,128)(2,1)S(1)}, u32[]{:S(2)}, u32[]{:S(2)}) collective-permute-start(bf16[32,512]{1,0:T(8,128)(2,1)} %get-tuple-element.14), channel_id=1, source_target_pairs={{0,2},{1,3},{2,0},{3,1},{4,6},{5,7},{6,4},{7,5},{8,10},{9,11},{10,... | collective-permute-start | bytes 98312 | tf_op jit(solution)/shard_map/ppermute | solution.py:21
  58.3 3.8 %collective-permute-start.14 = (bf16[16,512]{1,0:T(8,128)(2,1)S(1)}, bf16[16,512]{1,0:T(8,128)(2,1)S(1)}, u32[]{:S(2)}, u32[]{:S(2)}) collective-permute-start(bf16[16,512]{1,0:T(8,128)(2,1)S(1)} %dynamic-slice_convert_fusion), channel_id=1, source_target_pairs={{0,1},{1,0},{2,3},{3,2},{4,5},{5,4},{6,7},{7,6},{8,9},{9,8},{10,11... | collective-permute-start | bytes 49160 | tf_op jit(solution)/shard_map/ppermute | solution.py:21
  62.1 0.6 copy-start.15
